TPU v7x, 32 devices: a whole 2x2x4 slice. The times are simulated.
32 devices in a mesh: seq: 4 (over y, x), wshard: 8 (over z, core).
Axes of the slice: x: 2, y: 2, z: 4, core: 2. Of those that a mesh axis runs over, the one named last changes fastest.
Arguments:
- inputs: bfloat16 [8, 1024, 1024], P('wshard', 'seq'), may hold values from -6 to 6
- routes: int32 [8, 1024, 1], P('wshard', 'seq'), may hold values from 0 to 3; in each aligned block of 256 rows (0 to 255, 256 to 511, ..., all dimensions but the last counted through in order) at most 96 rows name the same one
- block_ids: int32 [8, 1024], P('wshard'), may hold values from 0 to 7, never falling along the last dimension, each value on 1 to 256 neighbouring positions
- qkv_weight: bfloat16 [1024, 3072], P('wshard'), may hold values from -0.1875 to 0.1875
- out_weight: bfloat16 [1024, 1024], P('wshard'), may hold values from -3 to 3
- gain_one: bfloat16 [1024], P('wshard'), may hold values from 0.5 to 1.5
- gain_two: bfloat16 [1024], P('wshard'), may hold values from 0.5 to 1.5
- centroid: bfloat16 [4, 1024], replicated, may hold values from -0.125 to 0.125
- up_one: bfloat16 [8, 2048, 1024], P('wshard', 'seq'), may hold values from -0.1875 to 0.1875
- down_one: bfloat16 [8, 2048, 1024], P('wshard', 'seq'), may hold values from -0.09375 to 0.09375
- up_two: bfloat16 [8, 2048, 1024], P('wshard', 'seq'), may hold values from -0.1875 to 0.1875
- down_two: bfloat16 [8, 2048, 1024], P('wshard', 'seq'), may hold values from -0.09375 to 0.09375
- cotangent: bfloat16 [8, 1024, 1024], P('wshard', 'seq'), may hold values from -6 to 6
Outputs:
- layer_out: bfloat16 [8, 1024, 1024], P('wshard', 'seq')
- input_grad: bfloat16 [8, 1024, 1024], P('wshard', 'seq')
- qkv_grad: float32 [1024, 3072], P('wshard')
- out_grad: float32 [1024, 1024], P('wshard')
- gain_one_grad: float32 [1024], P('wshard')
- gain_two_grad: float32 [1024], P('wshard')
- centroid_grad: float32 [4, 1024], replicated
- up_one_grad: float32 [8, 2048, 1024], P('wshard', 'seq')
- down_one_grad: float32 [8, 2048, 1024], P('wshard', 'seq')
- up_two_grad: float32 [8, 2048, 1024], P('wshard', 'seq')
- down_two_grad: float32 [8, 2048, 1024], P('wshard', 'seq')
Inputs may be any that keep to these rules, and one draw needn't show every extreme that they name: `routes`: among the 256 tokens of one device (aligned blocks of the flattened rows), no expert is named more than 96 times, and some device names one expert exactly 96 times. `block_ids`: along each sequence the block ids never fall, every id is used, each block spans 1 to 256 positions and one spans exactly 256.
All inputs are finite; a program needn't handle non-finite values.
Results may differ from a plain program's by a relative error of at most 0.015.
Values may be sent and summed in bfloat16 or wider, within the bound.
A program may use at most 256 MiB of HBM per device.

v0:
```python
import jax
import jax.numpy as jnp
from jax import lax
from jax.sharding import PartitionSpec as P

HEAD = 64


EPSILON = 1e-05
NEG_FILL = -1e30


def as_sent(shard):

    def short(part):
        return part.astype(jnp.bfloat16) if part.dtype == jnp.float32 else part

    return jax.tree.map(short, shard)


def from_partner(shard, axis, distance):
    return lax.ppermute(shard, axis, [(i, i ^ 1 << distance) for i in range(lax.axis_size(axis))])


def norm_rows(values, gain_vec):
    centre = jnp.mean(values, axis=-1, keepdims=True)
    shifted = values - centre
    spread = jnp.mean(shifted * shifted, axis=-1, keepdims=True)
    return shifted * lax.rsqrt(spread + EPSILON) * gain_vec


def gelu_exact(argument):
    return jax.nn.gelu(argument, approximate=False)


def gelu_back(pre_act, upstream):
    return jax.vjp(gelu_exact, pre_act)[1](upstream)[0]


def dot_rows(left_mat, right_mat):
    return lax.dot_general(
        left_mat, right_mat, (((0,), (0,)), ((), ())), preferred_element_type=jnp.float32
    )


def dot_last(left_mat, right_mat):
    return lax.dot_general(
        left_mat, right_mat, (((1,), (1,)), ((), ())), preferred_element_type=jnp.float32
    )


def heads_layout(parts_tuple):
    return jax.tree.map(
        lambda part, own: part.astype(own.dtype),
        lax.all_to_all(as_sent(parts_tuple), "seq", split_axis=1, concat_axis=0, tiled=True),
        parts_tuple,
    )


def tokens_layout(parts_tuple):
    return jax.tree.map(
        lambda part, own: part.astype(own.dtype),
        lax.all_to_all(as_sent(parts_tuple), "seq", split_axis=0, concat_axis=1, tiled=True),
        parts_tuple,
    )


def to_owner(slab_rows):
    return lax.all_to_all(slab_rows, "wshard", split_axis=0, concat_axis=0, tiled=True)


def from_owner(slab_rows):
    return lax.all_to_all(slab_rows, "wshard", split_axis=0, concat_axis=0, tiled=True)


def all_quarters(slab_rows):
    return lax.all_gather(slab_rows, "seq", axis=0, tiled=True)


def pair_sum(partial_sum):
    return partial_sum + from_partner(partial_sum, "wshard", 0)


def quarter_sum(partial_sum):
    return lax.psum_scatter(partial_sum, "seq", scatter_dimension=0, tiled=True)


def expert_view(slab_rows):
    return all_quarters(slab_rows)


def hidden_total(partial_sum):
    return quarter_sum(pair_sum(partial_sum))


def attend_forward(query_head, key_head, value_head, block_row, score_scale):
    length = query_head.shape[0]
    block_span = min(512, length)
    heads_here = query_head.shape[1] // HEAD
    keys_split = key_head.reshape(length, heads_here, HEAD)
    values_split = value_head.reshape(length, heads_here, HEAD)

    def one_block(start_row):
        query_part = lax.dynamic_slice_in_dim(query_head, start_row, block_span, 0).reshape(
            block_span, heads_here, HEAD
        )
        block_part = lax.dynamic_slice_in_dim(block_row, start_row, block_span, 0)
        scores = (
            jnp.einsum("qhc,khc->hqk", query_part, keys_split, preferred_element_type=jnp.float32)
            * score_scale
        )
        allowed = block_row[None, None, :] <= block_part[None, :, None]
        scores = jnp.where(allowed, scores, NEG_FILL)
        row_top = jnp.max(scores, axis=2, keepdims=True)
        weights = jnp.exp(scores - row_top)
        row_total = jnp.sum(weights, axis=2, keepdims=True)
        prob_low = (weights / row_total).astype(jnp.bfloat16)
        mixed_out = jnp.einsum(
            "hqk,khc->qhc", prob_low, values_split, preferred_element_type=jnp.float32
        )
        return (
            mixed_out.reshape(block_span, heads_here * HEAD).astype(jnp.bfloat16),
            (row_top + jnp.log(row_total))[:, :, 0],
        )

    starts = jnp.arange(length // block_span, dtype=jnp.int32) * block_span
    mixed_blocks, lse_blocks = lax.map(one_block, starts)
    return (
        mixed_blocks.reshape(length, heads_here * HEAD),
        jnp.transpose(lse_blocks, (1, 0, 2)).reshape(heads_here, length),
    )


def attend_backward(query_head, key_head, value_head, block_row, log_total, grad_head, score_scale):
    length = query_head.shape[0]
    block_span = min(512, length)
    heads_here = query_head.shape[1] // HEAD
    keys_split = key_head.reshape(length, heads_here, HEAD)
    values_split = value_head.reshape(length, heads_here, HEAD)

    def one_block(carry, start_row):
        key_acc, value_acc = carry
        query_part = lax.dynamic_slice_in_dim(query_head, start_row, block_span, 0).reshape(
            block_span, heads_here, HEAD
        )
        grad_part = lax.dynamic_slice_in_dim(grad_head, start_row, block_span, 0).reshape(
            block_span, heads_here, HEAD
        )
        block_part = lax.dynamic_slice_in_dim(block_row, start_row, block_span, 0)
        lse_part = lax.dynamic_slice_in_dim(log_total, start_row, block_span, 1)
        scores = (
            jnp.einsum("qhc,khc->hqk", query_part, keys_split, preferred_element_type=jnp.float32)
            * score_scale
        )
        allowed = block_row[None, None, :] <= block_part[None, :, None]
        scores = jnp.where(allowed, scores, NEG_FILL)
        prob_full = jnp.exp(scores - lse_part[:, :, None])
        prob_low = prob_full.astype(jnp.bfloat16)
        d_prob = jnp.einsum(
            "qhc,khc->hqk", grad_part, values_split, preferred_element_type=jnp.float32
        )
        row_dot = jnp.sum(prob_full * d_prob, axis=2, keepdims=True)
        d_scores = (prob_full * (d_prob - row_dot)).astype(jnp.bfloat16)
        d_query = (
            jnp.einsum("hqk,khc->qhc", d_scores, keys_split, preferred_element_type=jnp.float32)
            * score_scale
        )
        key_acc = (
            key_acc
            + jnp.einsum("hqk,qhc->khc", d_scores, query_part, preferred_element_type=jnp.float32)
            * score_scale
        )
        value_acc = value_acc + jnp.einsum(
            "hqk,qhc->khc", prob_low, grad_part, preferred_element_type=jnp.float32
        )
        return (
            (key_acc, value_acc),
            d_query.reshape(block_span, heads_here * HEAD).astype(jnp.bfloat16),
        )

    starts = jnp.arange(length // block_span, dtype=jnp.int32) * block_span
    zeros_acc = jnp.zeros((length, heads_here, HEAD), jnp.float32)
    (key_acc, value_acc), query_blocks = lax.scan(one_block, (zeros_acc, zeros_acc), starts)
    flat_width = heads_here * HEAD
    return (
        query_blocks.reshape(length, flat_width),
        key_acc.reshape(length, flat_width).astype(jnp.bfloat16),
        value_acc.reshape(length, flat_width).astype(jnp.bfloat16),
    )


def local(
    inputs,
    routes,
    block_ids,
    qkv_weight,
    out_weight,
    gain_one,
    gain_two,
    centroid,
    up_one,
    down_one,
    up_two,
    down_two,
    cotangent,
):
    tok_count = inputs.shape[1]
    model_width = inputs.shape[2]
    exp_count = centroid.shape[0]
    slot_most = max(2, 3 * tok_count // (2 * exp_count))
    local_capacity = max(1, 9 * tok_count // (8 * exp_count))
    score_scale = HEAD ** (-0.5)
    half_width = model_width // 2
    pair_bit = lax.axis_index("wshard") % 2
    full_qkv, full_out, full_gain_one, full_gain_two = (
        lax.all_gather(qkv_weight, "wshard", axis=0, tiled=True),
        lax.all_gather(out_weight, "wshard", axis=0, tiled=True),
        lax.all_gather(gain_one, "wshard", axis=0, tiled=True),
        lax.all_gather(gain_two, "wshard", axis=0, tiled=True),
    )
    gain_first = full_gain_one.astype(jnp.float32)
    gain_second = full_gain_two.astype(jnp.float32)
    tokens_in = inputs[0].astype(jnp.float32)
    normed_one = norm_rows(tokens_in, gain_first).astype(jnp.bfloat16)
    projected = jnp.dot(normed_one, full_qkv, preferred_element_type=jnp.float32).astype(
        jnp.bfloat16
    )
    query_head, key_head, value_head = heads_layout(
        (
            projected[:, :model_width],
            projected[:, model_width : 2 * model_width],
            projected[:, 2 * model_width :],
        )
    )
    block_row = block_ids[0]
    mixed_head, log_total = attend_forward(query_head, key_head, value_head, block_row, score_scale)
    (mixed_tok,) = tokens_layout((mixed_head,))
    hidden = tokens_in + jnp.dot(mixed_tok, full_out, preferred_element_type=jnp.float32)
    normed_two = norm_rows(hidden, gain_second).astype(jnp.bfloat16)
    route_ids = routes[0, :, 0]
    expert_ids = jnp.arange(exp_count, dtype=jnp.int32)
    expert_hot = route_ids[:, None] == expert_ids[None, :]
    hot_low = expert_hot.astype(jnp.bfloat16)
    logits = dot_last(normed_two, centroid)
    chosen = jnp.sum(jnp.where(expert_hot, logits, 0.0), axis=1)
    sigmoid_val = jax.nn.sigmoid(chosen)
    positions = jnp.arange(tok_count, dtype=jnp.int32)
    lower_tri = (positions[:, None] >= positions[None, :]).astype(jnp.bfloat16)
    running = jnp.dot(lower_tri, hot_low, preferred_element_type=jnp.float32)
    local_rank = (jnp.sum(jnp.where(expert_hot, running, 0.0), axis=1) - 1.0).astype(jnp.int32)
    kept_mask = local_rank < local_capacity
    gate_val = jnp.where(kept_mask, sigmoid_val, 0.0)
    slot_id = route_ids * slot_most + local_rank
    slot_ids = jnp.arange(exp_count * slot_most, dtype=jnp.int32)
    dispatch = ((slot_ids[:, None] == slot_id[None, :]) & kept_mask[None, :]).astype(jnp.bfloat16)

    def spread_out(token_rows):
        packed = jnp.dot(dispatch, token_rows, preferred_element_type=jnp.float32).astype(
            jnp.bfloat16
        )
        packed = packed.reshape(exp_count, 1, slot_most, model_width)
        doubled = jnp.broadcast_to(packed, (exp_count, 2, slot_most, model_width)).reshape(
            2 * exp_count, slot_most, model_width
        )
        return to_owner(doubled).reshape(-1, model_width)

    def gather_back(own_rows):
        own_half = lax.dynamic_slice_in_dim(own_rows, pair_bit * half_width, half_width, 1)
        returned = from_owner(own_half.reshape(2 * exp_count, slot_most, half_width))
        paired = returned.reshape(exp_count, 2, slot_most, half_width)
        joined = jnp.concatenate((paired[:, 0], paired[:, 1]), axis=2).reshape(
            exp_count * slot_most, model_width
        )
        return dot_rows(dispatch, joined)

    up_a, down_a, up_b, down_b = (up_one[0], down_one[0], up_two[0], down_two[0])
    sent_own = spread_out(normed_two)
    sent_all = expert_view(sent_own)
    pre_one = dot_last(sent_all, up_a)
    act_one = gelu_exact(pre_one).astype(jnp.bfloat16)
    first_own = (
        sent_own.astype(jnp.float32)
        + hidden_total(jnp.dot(act_one, down_a, preferred_element_type=jnp.float32))
    ).astype(jnp.bfloat16)
    first_all = expert_view(first_own)
    pre_two = dot_last(first_all, up_b)
    act_two = gelu_exact(pre_two).astype(jnp.bfloat16)
    second_own = (
        first_own.astype(jnp.float32)
        + hidden_total(jnp.dot(act_two, down_b, preferred_element_type=jnp.float32))
    ).astype(jnp.bfloat16)
    returned_tok = gather_back(second_own)
    layer_out = (hidden + gate_val[:, None] * returned_tok).astype(jnp.bfloat16)
    dy_rows = cotangent[0].astype(jnp.float32)
    d_gate = jnp.where(kept_mask, jnp.sum(dy_rows * returned_tok, axis=1), 0.0)
    d_chosen = d_gate * sigmoid_val * (1.0 - sigmoid_val)
    d_second_own = spread_out((gate_val[:, None] * dy_rows).astype(jnp.bfloat16))
    d_second_all = expert_view(d_second_own)
    d_pre_two = gelu_back(pre_two, dot_last(d_second_all, down_b)).astype(jnp.bfloat16)
    d_first_own = (
        d_second_own.astype(jnp.float32)
        + hidden_total(jnp.dot(d_pre_two, up_b, preferred_element_type=jnp.float32))
    ).astype(jnp.bfloat16)
    d_first_all = expert_view(d_first_own)
    d_pre_one = gelu_back(pre_one, dot_last(d_first_all, down_a)).astype(jnp.bfloat16)
    d_sent_own = (
        d_first_own.astype(jnp.float32)
        + hidden_total(jnp.dot(d_pre_one, up_a, preferred_element_type=jnp.float32))
    ).astype(jnp.bfloat16)
    grad_stack = jnp.stack(
        (
            dot_rows(d_pre_one, sent_all),
            dot_rows(act_one, d_first_all),
            dot_rows(d_pre_two, first_all),
            dot_rows(act_two, d_second_all),
        ),
        axis=1,
    )
    d_sent_tok = gather_back(d_sent_own)
    centroid_tok = jnp.dot(hot_low, centroid, preferred_element_type=jnp.float32)
    d_normed_two = d_sent_tok + d_chosen[:, None] * centroid_tok
    centroid_term = lax.dot_general(
        expert_hot.astype(jnp.float32),
        d_chosen[:, None] * normed_two.astype(jnp.float32),
        (((0,), (0,)), ((), ())),
        precision=lax.Precision.HIGHEST,
        preferred_element_type=jnp.float32,
    )
    grad_centroid = lax.psum(centroid_term, ("seq", "wshard"))
    norm_two_back = jax.vjp(norm_rows, hidden, gain_second)[1]
    d_hidden_norm, d_gain_second = norm_two_back(d_normed_two)
    d_hidden = dy_rows + d_hidden_norm
    d_branch = d_hidden.astype(jnp.bfloat16)
    grad_out_full = dot_rows(mixed_tok, d_branch)
    d_mixed = dot_last(d_branch, full_out).astype(jnp.bfloat16)
    (d_mixed_head,) = heads_layout((d_mixed,))
    d_query, d_key, d_value = attend_backward(
        query_head, key_head, value_head, block_row, log_total, d_mixed_head, score_scale
    )
    d_query_tok, d_key_tok, d_value_tok = tokens_layout((d_query, d_key, d_value))
    d_projected = jnp.concatenate((d_query_tok, d_key_tok, d_value_tok), axis=1)
    grad_qkv_full = dot_rows(normed_one, d_projected)
    d_normed_one = dot_last(d_projected, full_qkv)
    norm_one_back = jax.vjp(norm_rows, tokens_in, gain_first)[1]
    d_tokens_norm, d_gain_first = norm_one_back(d_normed_one)
    input_grad = (d_hidden + d_tokens_norm).astype(jnp.bfloat16)
    qkv_part, out_part, gain_first_part, gain_second_part = (
        lax.psum_scatter(grad_qkv_full, "wshard", scatter_dimension=0, tiled=True),
        lax.psum_scatter(grad_out_full, "wshard", scatter_dimension=0, tiled=True),
        lax.psum_scatter(d_gain_first, "wshard", scatter_dimension=0, tiled=True),
        lax.psum_scatter(d_gain_second, "wshard", scatter_dimension=0, tiled=True),
    )
    grad_qkv, grad_out, grad_gain_one, grad_gain_two = (
        lax.psum(qkv_part.astype(jnp.bfloat16), "seq").astype(jnp.float32),
        lax.psum(out_part.astype(jnp.bfloat16), "seq").astype(jnp.float32),
        lax.psum(gain_first_part.astype(jnp.bfloat16), "seq").astype(jnp.float32),
        lax.psum(gain_second_part.astype(jnp.bfloat16), "seq").astype(jnp.float32),
    )
    return (
        layer_out[None],
        input_grad[None],
        grad_qkv,
        grad_out,
        grad_gain_one,
        grad_gain_two,
        grad_centroid,
        grad_stack[:, 0][None],
        grad_stack[:, 1][None],
        grad_stack[:, 2][None],
        grad_stack[:, 3][None],
    )


def solution(mesh):
    return jax.shard_map(
        local,
        mesh=mesh,
        in_specs=(
            P("wshard", "seq", None),
            P("wshard", "seq", None),
            P("wshard", None),
            P("wshard", None),
            P("wshard", None),
            P("wshard"),
            P("wshard"),
            P(),
            P("wshard", "seq", None),
            P("wshard", "seq", None),
            P("wshard", "seq", None),
            P("wshard", "seq", None),
            P("wshard", "seq", None),
        ),
        out_specs=(
            P("wshard", "seq", None),
            P("wshard", "seq", None),
            P("wshard", None),
            P("wshard", None),
            P("wshard"),
            P("wshard"),
            P(),
            P("wshard", "seq", None),
            P("wshard", "seq", None),
            P("wshard", "seq", None),
            P("wshard", "seq", None),
        ),
        check_vma=False,
    )
```

profile of v0, /device:TPU:14, one launch (start us, length us, event | category | flops | bytes accessed | tf_op | source)
XLA Modules:
  0.0 1420.4 jit_solution(8073177528642186670)
XLA Ops:
  7.9 9.2 all-gather
  20.3 53.1 %all-gather.9.cloned.1.call-done = bf16[1024,3072]{1,0:T(8,128)(2,1)} async-done(((bf16[128,3072]{1,0:T(8,128)(2,1)}), bf16[1024,3072]{1,0:T(8,128)(2,1)}) %all-gather.9.cloned.1.call-update) | async-done | bytes 6291472 | tf_op jit(solution)/shard_map/all_gather | solution.py:216
  84.3 6.2 all-to-all-done.1
  113.7 25.3 %while.27 = (s32[]{:T(128)}, bf16[2,512,256]{2,1,0:T(8,128)(2,1)}, f32[2,4,512]{2,1,0:T(4,128)S(1)}, s32[1,1024]{1,0:T(1,128)S(1)}, s32[2]{0:T(128)}, /*index=5*...) while((s32[]{:T(128)}, bf16[2,512,256]{2,1,0:T(8,128)(2,1)}, ...), condition=%wide.region_5.6_spmd, body=%wide.region_2.5_spmd.sunk | while | flops 562690048 | bytes 30485168 | solution.py:127
  144.1 10.9 all-gather.1
  162.6 39.5 %all_to_all.160 = bf16[8,96,1024]{2,1,0:T(8,128)(2,1)} all-to-all(bf16[8,96,1024]{2,1,0:T(8,128)(2,1)S(1)} %bitcast.275), channel_id=1, replica_groups=mesh['seq'=4,'wshard'=8] {'wshard'}, dimensions={0} | all-to-all | bytes 3145728 | tf_op jit(solution)/shard_map/all_to_all | solution.py:69
  202.3 69.6 %all-gather.13.cloned.1.call-done = bf16[3072,1024]{1,0:T(8,128)(2,1)} async-done(((bf16[768,1024]{1,0:T(8,128)(2,1)}), bf16[3072,1024]{1,0:T(8,128)(2,1)}) %all-gather.13.cloned.1.call-update) | async-done | bytes 6291472 | tf_op jit(solution)/shard_map/all_gather | solution.py:77
  272.0 19.9 %multiply_convert_fusion.2 = (bf16[3072,512]{1,0:T(8,128)(2,1)S(1)}, f32[3072,512]{1,0:T(8,128)}, f32[3072,512]{1,0:T(8,128)}) fusion(bf16[3072,1024]{1,0:T(8,128)(2,1)} %all-gather.13.cloned.1.call-done, bf16[1,512,1024]{2,1,0:T(8,128)(2,1)} %param.25), kind=kOutput, calls=%fused_computation.52 | convolution fusion | flops 3323461632 | bytes 23068672 | tf_op jit(solution)/shard_map/dot_general | solution.py:47
  295.4 19.1 %collective-permute-done = f32[3072,1024]{1,0:T(8,128)S(1)} collective-permute-done((f32[3072,1024]{1,0:T(8,128)S(1)}, f32[3072,1024]{1,0:T(8,128)S(1)}, u32[]{:S(2)}, u32[]{:S(2)}) %collective-permute-start) | collective-permute-done | bytes 12582944 | tf_op jit(solution)/shard_map/ppermute | solution.py:22
  314.5 6.0 add.169
  320.7 120.7 %reduce-scatter.7.cloned.1.call-done = f32[768,1024]{1,0:T(8,128)} async-done(((f32[3072,1024]{1,0:T(8,128)}), f32[768,1024]{1,0:T(8,128)}) %reduce-scatter.7.cloned.1.call-update) | async-done | bytes 3145744 | tf_op jit(solution)/shard_map/reduce_scatter | solution.py:85
  445.7 40.6 %all_to_all.161 = bf16[8,96,1024]{2,1,0:T(8,128)(2,1)} all-to-all(bf16[8,96,1024]{2,1,0:T(8,128)(2,1)S(1)} %bitcast.276), channel_id=1, replica_groups=mesh['seq'=4,'wshard'=8] {'wshard'}, dimensions={0} | all-to-all | bytes 3145728 | tf_op jit(solution)/shard_map/all_to_all | solution.py:69
  486.6 28.6 %all-gather.15.cloned.1.call-done = bf16[3072,1024]{1,0:T(8,128)(2,1)} async-done(((bf16[768,1024]{1,0:T(8,128)(2,1)}), bf16[3072,1024]{1,0:T(8,128)(2,1)}) %all-gather.15.cloned.1.call-update) | async-done | bytes 6291472 | tf_op jit(solution)/shard_map/all_gather | solution.py:77
  515.2 19.9 %multiply_convert_fusion.1 = (bf16[3072,512]{1,0:T(8,128)(2,1)}, f32[3072,512]{1,0:T(8,128)}, f32[3072,512]{1,0:T(8,128)}) fusion(bf16[3072,1024]{1,0:T(8,128)(2,1)} %all-gather.15.cloned.1.call-done, bf16[1,512,1024]{2,1,0:T(8,128)(2,1)S(1)} %copy-done), kind=kOutput, calls=%fused_computation.39 | convolution fusion | flops 3323461632 | bytes 23068672 | tf_op jit(solution)/shard_map/dot_general | solution.py:47
  535.1 51.9 %all-gather.17.cloned.1.call-done = bf16[3072,1024]{1,0:T(8,128)(2,1)} async-done(((bf16[768,1024]{1,0:T(8,128)(2,1)}), bf16[3072,1024]{1,0:T(8,128)(2,1)}) %all-gather.17.cloned.1.call-update) | async-done | bytes 6291472 | tf_op jit(solution)/shard_map/all_gather | solution.py:77
  586.9 9.9 add_convert_fusion.1
  602.1 19.1 %collective-permute-done.2 = f32[3072,1024]{1,0:T(8,128)S(1)} collective-permute-done((f32[3072,1024]{1,0:T(8,128)S(1)}, f32[3072,1024]{1,0:T(8,128)S(1)}, u32[]{:S(2)}, u32[]{:S(2)}) %collective-permute-start.2) | collective-permute-done | bytes 12582944 | tf_op jit(solution)/shard_map/ppermute | solution.py:22
  621.2 6.1 add.176
  628.5 8.8 fusion.52
  637.5 110.6 %reduce-scatter.11.cloned.1.call-done = f32[768,1024]{1,0:T(8,128)} async-done(((f32[3072,1024]{1,0:T(8,128)}), f32[768,1024]{1,0:T(8,128)}) %reduce-scatter.11.cloned.1.call-update) | async-done | bytes 3145744 | tf_op jit(solution)/shard_map/reduce_scatter | solution.py:85
  751.8 15.4 %add.171 = f32[3072,1024]{1,0:T(8,128)} add(f32[3072,1024]{1,0:T(8,128)} %fusion.52, f32[3072,1024]{1,0:T(8,128)} %collective-permute-done.1) | non-fusion elementwise | flops 3145728 | bytes 37748736 | tf_op jit(solution)/shard_map/add | solution.py:81
  767.3 54.6 %all-gather.19.cloned.1.call-done = bf16[3072,1024]{1,0:T(8,128)(2,1)} async-done(((bf16[768,1024]{1,0:T(8,128)(2,1)}), bf16[3072,1024]{1,0:T(8,128)(2,1)}) %all-gather.19.cloned.1.call-update) | async-done | bytes 6291472 | tf_op jit(solution)/shard_map/all_gather | solution.py:77
  821.9 10.0 add_convert_fusion
  837.5 19.1 %collective-permute-done.3 = f32[3072,1024]{1,0:T(8,128)S(1)} collective-permute-done((f32[3072,1024]{1,0:T(8,128)S(1)}, f32[3072,1024]{1,0:T(8,128)S(1)}, u32[]{:S(2)}, u32[]{:S(2)}) %collective-permute-start.3) | collective-permute-done | bytes 12582944 | tf_op jit(solution)/shard_map/ppermute | solution.py:22
  856.6 6.0 add.178
  862.8 82.9 %reduce-scatter.9.cloned.1.call-done = f32[768,1024]{1,0:T(8,128)} async-done(((f32[3072,1024]{1,0:T(8,128)}), f32[768,1024]{1,0:T(8,128)}) %reduce-scatter.9.cloned.1.call-update) | async-done | bytes 3145744 | tf_op jit(solution)/shard_map/reduce_scatter | solution.py:85
  953.5 115.7 %reduce-scatter.13.cloned.1.call-done = f32[768,1024]{1,0:T(8,128)} async-done(((f32[3072,1024]{1,0:T(8,128)}), f32[768,1024]{1,0:T(8,128)}) %reduce-scatter.13.cloned.1.call-update) | async-done | bytes 3145744 | tf_op jit(solution)/shard_map/reduce_scatter | solution.py:85
  1072.0 5.4 all-to-all-start.7
  1079.3 15.5 %all-to-all-done.7 = bf16[8,96,512]{2,1,0:T(8,128)(2,1)} async-done(((bf16[8,96,512]{2,1,0:T(8,128)(2,1)}), bf16[8,96,512]{2,1,0:T(8,128)(2,1)}, u32[]{:S(2)}, u32[]{:S(2)}) %all-to-all-start.7) | async-done | bytes 786464 | tf_op jit(solution)/shard_map/all_to_all | solution.py:73
  1102.8 5.6 all-to-all-start.8
  1116.4 69.4 %while.28 = (s32[]{:T(128)}, f32[1024,4,64]{0,2,1:T(8,128)S(1)}, f32[1024,4,64]{0,2,1:T(8,128)}, bf16[2,512,256]{2,1,0:T(8,128)(2,1)}, s32[2]{0:T(128)}, /*index...) while((s32[]{:T(128)}, f32[1024,4,64]{0,2,1:T(8,128)S(1)}, ...), condition=%wide.region_19.20_spmd.clone, body=%wide.region_17.19_spmd.clone.sunk | while | flops 1375729664 | bytes 93653776 | solution.py:183
  1127.0 5.7 multiply_reduce_fusion.5
  1145.1 6.0 fusion.201
  1161.7 5.6 multiply_reduce_fusion.5
  1179.6 6.2 fusion.201
  1186.3 10.0 all_to_all.162
  1196.3 5.5 all-to-all-start.9
  1217.0 6.7 fusion.81
  1225.5 8.6 convolution_bitcast_fusion.1
  1234.2 7.7 convolution_bitcast_fusion
  1242.4 44.8 %psum.39 = f32[4,1024]{1,0:T(4,128)} all-reduce(f32[4,1024]{1,0:T(4,128)S(1)} %fusion.70), channel_id=1, replica_groups=mesh['seq'=4,'wshard'=8] {'seq','wshard'}, use_global_device_ids=true, to_apply=%region_32.33 | all-reduce | flops 4096 | bytes 32768 | tf_op jit(solution)/shard_map/psum | solution.py:329
  1287.2 8.7 convolution_bitcast_fusion.2
  1295.8 7.6 convolution_bitcast_fusion.3
  1305.3 47.9 %reduce-scatter.15.cloned.1.call-done = f32[128,3072]{1,0:T(8,128)} async-done(((f32[1024,3072]{1,0:T(8,128)}), f32[128,3072]{1,0:T(8,128)}) %reduce-scatter.15.cloned.1.call-update) | async-done | bytes 1572880 | tf_op jit(solution)/shard_map/reduce_scatter | solution.py:348
  1355.6 5.4 fusion.47
  1362.6 13.3 all-reduce.2
  1376.0 8.1 all-reduce.3
  1387.6 21.6 %all-reduce.7.cloned.1.call-done = (bf16[128,3072]{1,0:T(8,128)(2,1)}, bf16[128,1024]{1,0:T(8,128)(2,1)}) async-done(((bf16[128,3072]{1,0:T(8,128)(2,1)}, bf16[128,1024]{1,0:T(8,128)(2,1)}), (bf16[128,3072]{1,0:T(8,128)(2,1)}, bf16[128,1024]{1,0:T(8,128)(2,1)})) %all-reduce.7.cloned.1.call-update) | async-done | bytes 1048592 | tf_op jit(solution)/shard_map/psum | solution.py:354
  (327 shorter events, 197.3 us)
Async XLA Ops:
  7.2 508.0 %copy-start = (bf16[1,512,1024]{2,1,0:T(8,128)(2,1)S(1)}, bf16[1,512,1024]{2,1,0:T(8,128)(2,1)}, u32[]{:S(2)}) copy-start(bf16[1,512,1024]{2,1,0:T(8,128)(2,1)} %param.27) | copy-start | bytes 3145732
  7.2 66.2 %all-gather.9.cloned.1.call-start = ((), (), s32[]{:S(2)}) async-start(), calls=%async_computation.18 | async-start | bytes 7077888 | tf_op jit(solution)/shard_map/all_gather | solution.py:216
  17.1 61.1 %copy-start.32 = (f32[8,1,128]{2,1,0:T(1,128)}, f32[8,1,128]{2,1,0:T(1,128)S(1)}, u32[]{:S(2)}) copy-start(f32[8,1,128]{2,1,0:T(1,128)S(1)} %convert_element_type.230) | copy-start | bytes 12292
  18.4 59.9 %copy-start.38 = (f32[256]{0:T(256)}, f32[256]{0:T(256)S(1)}, u32[]{:S(2)}) copy-start(f32[256]{0:T(256)S(1)} %broadcast_multiply_fusion.1) | copy-start | bytes 3076
  79.3 11.2 all-to-all-start.1
  90.5 11.1 all-to-all-start.2
  101.6 10.3 all-to-all-start
  106.5 50.8 %all-gather.11.cloned.1.call-start = ((), (), s32[]{:S(2)}) async-start(), calls=%async_computation.19 | async-start | bytes 2359296 | tf_op jit(solution)/shard_map/all_gather | solution.py:217
  139.0 16.3 %all-to-all-start.3 = ((bf16[4,256,256]{2,1,0:T(8,128)(2,1)}), bf16[4,256,256]{2,1,0:T(8,128)(2,1)S(1)}, u32[]{:S(2)}, u32[]{:S(2)}) async-start(bf16[4,256,256]{2,1,0:T(8,128)(2,1)} %bitcast.288), calls=%async_computation.3 | async-start | bytes 1048576 | tf_op jit(solution)/shard_map/all_to_all | solution.py:63
  144.1 127.9 %all-gather.13.cloned.1.call-start = ((), (), s32[]{:S(2)}) async-start(), calls=%async_computation.20 | async-start | bytes 7864320 | tf_op jit(solution)/shard_map/all_gather | solution.py:77
  155.2 289.8 %copy-start.49 = (s32[256]{0:T(256)}, s32[256]{0:T(256)S(1)}, u32[]{:S(2)}) copy-start(s32[256]{0:T(256)S(1)} %multiply_add_fusion) | copy-start | bytes 3076
  161.9 283.1 %copy-start.53 = (pred[256]{0:T(512)(128)(4,1)}, pred[256]{0:T(512)(128)(4,1)S(1)}, u32[]{:S(2)}) copy-start(pred[256]{0:T(512)(128)(4,1)S(1)} %get-tuple-element.264) | copy-start | bytes 772
  161.9 283.1 %copy-start.61 = (f32[256]{0:T(256)}, f32[256]{0:T(256)S(1)}, u32[]{:S(2)}) copy-start(f32[256]{0:T(256)S(1)} %get-tuple-element.263) | copy-start | bytes 3076
  202.1 89.8 %copy-start.68 = (bf16[1,512,1024]{2,1,0:T(8,128)(2,1)S(1)}, bf16[1,512,1024]{2,1,0:T(8,128)(2,1)}, u32[]{:S(2)}) copy-start(bf16[1,512,1024]{2,1,0:T(8,128)(2,1)} %param.26) | copy-start | bytes 3145732
  202.1 239.3 %reduce-scatter.7.cloned.1.call-start = ((), (), s32[]{:S(2)}) async-start(), calls=%async_computation.21 | async-start | bytes 15728640 | tf_op jit(solution)/shard_map/reduce_scatter | solution.py:85
  295.3 19.2 %collective-permute-start = (f32[3072,1024]{1,0:T(8,128)S(1)}, f32[3072,1024]{1,0:T(8,128)S(1)}, u32[]{:S(2)}, u32[]{:S(2)}) collective-permute-start(f32[3072,1024]{1,0:T(8,128)S(1)} %fusion.62), channel_id=1, source_target_pairs={{0,1},{1,0},{2,3},{3,2},{4,5},{5,4},{6,7},{7,6},{8,9},{9,8},{10,11... | collective-permute-start | bytes 37748744 | tf_op jit(solution)/shard_map/ppermute | solution.py:22
  320.6 120.8 %copy-start.13 = (bf16[8,96,1024]{2,1,0:T(8,128)(2,1)S(1)}, bf16[8,96,1024]{2,1,0:T(8,128)(2,1)}, u32[]{:S(2)}) copy-start(bf16[8,96,1024]{2,1,0:T(8,128)(2,1)} %all_to_all.160) | copy-start | bytes 4718596
  320.6 124.5 %copy-start.21 = (bf16[1,256,1024]{2,1,0:T(8,128)(2,1)S(1)}, bf16[1,256,1024]{2,1,0:T(8,128)(2,1)}, u32[]{:S(2)}) copy-start(bf16[1,256,1024]{2,1,0:T(8,128)(2,1)} %param.29) | copy-start | bytes 1572868
  320.6 194.6 %all-gather.15.cloned.1.call-start = ((), (), s32[]{:S(2)}) async-start(), calls=%async_computation.22 | async-start | bytes 7864320 | tf_op jit(solution)/shard_map/all_gather | solution.py:77
  445.0 142.0 %all-gather.17.cloned.1.call-start = ((), (), s32[]{:S(2)}) async-start(), calls=%async_computation.24 | async-start | bytes 7864320 | tf_op jit(solution)/shard_map/all_gather | solution.py:77
  486.3 100.6 %copy-start.66 = (bf16[1,512,1024]{2,1,0:T(8,128)(2,1)S(1)}, bf16[1,512,1024]{2,1,0:T(8,128)(2,1)}, u32[]{:S(2)}) copy-start(bf16[1,512,1024]{2,1,0:T(8,128)(2,1)} %param.28) | copy-start | bytes 3145732
  486.3 261.8 %reduce-scatter.11.cloned.1.call-start = ((), (), s32[]{:S(2)}) async-start(), calls=%async_computation.25 | async-start | bytes 15728640 | tf_op jit(solution)/shard_map/reduce_scatter | solution.py:85
  602.0 19.2 %collective-permute-start.2 = (f32[3072,1024]{1,0:T(8,128)S(1)}, f32[3072,1024]{1,0:T(8,128)S(1)}, u32[]{:S(2)}, u32[]{:S(2)}) collective-permute-start(f32[3072,1024]{1,0:T(8,128)S(1)} %fusion.56), channel_id=1, source_target_pairs={{0,1},{1,0},{2,3},{3,2},{4,5},{5,4},{6,7},{7,6},{8,9},{9,8},{10,11... | collective-permute-start | bytes 37748744 | tf_op jit(solution)/shard_map/ppermute | solution.py:22
  627.3 194.6 %all-gather.19.cloned.1.call-start = ((), (), s32[]{:S(2)}) async-start(), calls=%async_computation.26 | async-start | bytes 7864320 | tf_op jit(solution)/shard_map/all_gather | solution.py:77
  628.5 119.6 %copy-start.12 = (bf16[8,96,1024]{2,1,0:T(8,128)(2,1)S(1)}, bf16[8,96,1024]{2,1,0:T(8,128)(2,1)}, u32[]{:S(2)}) copy-start(bf16[8,96,1024]{2,1,0:T(8,128)(2,1)} %all_to_all.161) | copy-start | bytes 4718596
  637.3 114.4 %collective-permute-start.1 = (f32[3072,1024]{1,0:T(8,128)}, f32[3072,1024]{1,0:T(8,128)}, u32[]{:S(2)}, u32[]{:S(2)}) collective-permute-start(f32[3072,1024]{1,0:T(8,128)} %fusion.52), channel_id=1, source_target_pairs={{0,1},{1,0},{2,3},{3,2},{4,5},{5,4},{6,7},{7,6},{8,9},{9,8},{10,11... | collective-permute-start | bytes 37748744 | tf_op jit(solution)/shard_map/ppermute | solution.py:22
  751.7 193.9 %reduce-scatter.9.cloned.1.call-start = ((), (), s32[]{:S(2)}) async-start(), calls=%async_computation.23 | async-start | bytes 15728640 | tf_op jit(solution)/shard_map/reduce_scatter | solution.py:85
  767.2 302.0 %reduce-scatter.13.cloned.1.call-start = ((), (), s32[]{:S(2)}) async-start(), calls=%async_computation.27 | async-start | bytes 15728640 | tf_op jit(solution)/shard_map/reduce_scatter | solution.py:85
  837.4 19.2 %collective-permute-start.3 = (f32[3072,1024]{1,0:T(8,128)S(1)}, f32[3072,1024]{1,0:T(8,128)S(1)}, u32[]{:S(2)}, u32[]{:S(2)}) collective-permute-start(f32[3072,1024]{1,0:T(8,128)S(1)} %fusion.66), channel_id=1, source_target_pairs={{0,1},{1,0},{2,3},{3,2},{4,5},{5,4},{6,7},{7,6},{8,9},{9,8},{10,11... | collective-permute-start | bytes 37748744 | tf_op jit(solution)/shard_map/ppermute | solution.py:22
  862.7 83.0 %copy-start.14 = (bf16[768,1024]{1,0:T(8,128)(2,1)S(1)}, bf16[768,1024]{1,0:T(8,128)(2,1)}, u32[]{:S(2)}) copy-start(bf16[768,1024]{1,0:T(8,128)(2,1)} %add_convert_fusion.3) | copy-start | bytes 4718596
  862.7 214.8 %copy-start.22 = (bf16[1,256,1024]{2,1,0:T(8,128)(2,1)S(1)}, bf16[1,256,1024]{2,1,0:T(8,128)(2,1)}, u32[]{:S(2)}) copy-start(bf16[1,256,1024]{2,1,0:T(8,128)(2,1)} %param.29) | copy-start | bytes 1572868
  862.7 214.8 %copy-start.50 = (s32[256]{0:T(256)S(1)}, s32[256]{0:T(256)}, u32[]{:S(2)}) copy-start(s32[256]{0:T(256)} %copy-done.49) | copy-start | bytes 3076
  862.7 214.8 %copy-start.54 = (pred[256]{0:T(512)(128)(4,1)S(1)}, pred[256]{0:T(512)(128)(4,1)}, u32[]{:S(2)}) copy-start(pred[256]{0:T(512)(128)(4,1)} %copy-done.53) | copy-start | bytes 772
  862.7 216.2 %copy-start.56 = (f32[256]{0:T(256)S(1)}, f32[256]{0:T(256)}, u32[]{:S(2)}) copy-start(f32[256]{0:T(256)} %copy-done.55) | copy-start | bytes 3076
  862.7 216.2 %copy-start.43 = (bf16[4,1024]{1,0:T(4,128)(2,1)S(1)}, bf16[4,1024]{1,0:T(4,128)(2,1)}, u32[]{:S(2)}) copy-start(bf16[4,1024]{1,0:T(4,128)(2,1)} %param.24) | copy-start | bytes 24580
  862.8 216.2 %copy-start.48 = (s32[1,256,1]{1,2,0:T(1,128)S(1)}, s32[1,256,1]{1,2,0:T(1,128)}, u32[]{:S(2)}) copy-start(s32[1,256,1]{1,2,0:T(1,128)} %param.18) | copy-start | bytes 3076
  948.2 147.9 %copy-start.6 = (f32[256,1024]{1,0:T(8,128)S(1)}, f32[256,1024]{1,0:T(8,128)}, u32[]{:S(2)}) copy-start(f32[256,1024]{1,0:T(8,128)} %copy-done.5) | copy-start | bytes 3145732
  948.2 147.9 %copy-start.37 = (f32[8,1,128]{2,1,0:T(1,128)S(1)}, f32[8,1,128]{2,1,0:T(1,128)}, u32[]{:S(2)}) copy-start(f32[8,1,128]{2,1,0:T(1,128)} %copy-done.36) | copy-start | bytes 12292
  948.2 147.9 %copy-start.45 = (f32[256]{0:T(256)S(1)}, f32[256]{0:T(256)}, u32[]{:S(2)}) copy-start(f32[256]{0:T(256)} %copy-done.44) | copy-start | bytes 3076
  948.2 147.9 %copy-start.52 = (f32[256]{0:T(256)S(1)}, f32[256]{0:T(256)}, u32[]{:S(2)}) copy-start(f32[256]{0:T(256)} %copy-done.51) | copy-start | bytes 3076
  948.2 123.7 %all-to-all-start.5 = ((bf16[8,96,512]{2,1,0:T(8,128)(2,1)}), bf16[8,96,512]{2,1,0:T(8,128)(2,1)S(1)}, u32[]{:S(2)}, u32[]{:S(2)}) async-start(bf16[8,96,512]{2,1,0:T(8,128)(2,1)} %bitcast.281), calls=%async_computation.7 | async-start | bytes 1572864 | tf_op jit(solution)/shard_map/all_to_all | solution.py:73
  1072.0 22.8 %all-to-all-start.7 = ((bf16[8,96,512]{2,1,0:T(8,128)(2,1)}), bf16[8,96,512]{2,1,0:T(8,128)(2,1)}, u32[]{:S(2)}, u32[]{:S(2)}) async-start(bf16[8,96,512]{2,1,0:T(8,128)(2,1)} %bitcast.280), calls=%async_computation.11 | async-start | bytes 1572864 | tf_op jit(solution)/shard_map/all_to_all | solution.py:73
  1102.8 12.7 all-to-all-start.8
  1108.4 195.1 %reduce-scatter.17.cloned.1.call-start = ((), (), s32[]{:S(2)}) async-start(), calls=%async_computation.29 | async-start | bytes 4718592 | tf_op jit(solution)/shard_map/reduce_scatter | solution.py:349
  1196.3 10.6 all-to-all-start.9
  1206.9 10.0 all-to-all-start.11
  1211.8 141.3 %reduce-scatter.15.cloned.1.call-start = ((), (), s32[]{:S(2)}) async-start(), calls=%async_computation.28 | async-start | bytes 14155776 | tf_op jit(solution)/shard_map/reduce_scatter | solution.py:348
  1223.7 185.5 %all-reduce.7.cloned.1.call-start = ((), (), s32[]{:S(2)}) async-start(), calls=%async_computation.30 | async-start | bytes 2097152 | tf_op jit(solution)/shard_map/psum | solution.py:354
  (57 other events, 960.8 us)
Sparse Core Ops, SparseCore 0:
  9.6 63.7 all-gather.8
  108.9 29.8 all-gather.10
  202.2 69.7 all-gather.12
  320.7 120.5 reduce-scatter.6
  445.1 70.0 all-gather.14
  516.9 70.0 all-gather.16
  627.4 120.6 reduce-scatter.10
  751.8 70.0 all-gather.18
  825.0 120.6 reduce-scatter.8
  948.6 120.5 reduce-scatter.12
  1111.5 48.6 reduce-scatter.16
  1223.8 129.3 reduce-scatter.14
  1356.2 52.9 all-reduce.6
where the time goes:
time: 1430 us; the launch traced here: 1420 us
  waiting for transfers between devices  857 us (60%)
  matrix products  190 us (13%)
  blocking collectives  176 us (12%)
  other arithmetic  82.1 us (6%)
  starting transfers between devices  47.5 us (3%)
  local copies, waits for them, and re-layouts  42.7 us (3%)
  between operations  15.9 us (1%)
    reduce_scatter x4, waiting for transfers between devices, quarter_sum(): return lax.psum_scatter(partial_sum, 'seq', scatter_dimension=0, tiled=True)  430 us
    all_gather x4, waiting for transfers between devices, all_quarters(): return lax.all_gather(slab_rows, 'seq', axis=0, tiled=True)  205 us
    all_to_all x2, blocking collectives, to_owner(): lax.all_to_all(slab_rows, 'wshard', split_axis=0, concat_axis=0, tiled=True)  80 us
    dot_general x7, matrix products, dot_last(): lax.dot_general(left_mat, right_mat, (((1,), (1,)), ((), ())), preferred_...  66.1 us
    ppermute x4, waiting for transfers between devices, from_partner(): lax.ppermute(shard, axis, [(i, i ^ 1 << distance) for i in range(lax.axis...  57.4 us
    all_gather x1, waiting for transfers between devices, local(): lax.all_gather(qkv_weight, 'wshard', axis=0, tiled=True)  53.1 us
    reduce_scatter x1, waiting for transfers between devices, local(): lax.psum_scatter(grad_qkv_full, 'wshard', scatter_dimension=0, tiled=True)  47.9 us
    psum x1, blocking collectives, local(): grad_centroid = lax.psum(centroid_term, ('seq', 'wshard'))  44.8 us
  transfers between devices with their start and end apart: 26, of which 21 were waited for; matrix products, arithmetic and copies ran while one was open for 16% of the time, Pallas kernels for 0%

commit v1 on v0

--- a/solution.py
+++ b/solution.py
@@ -63,34 +63,6 @@
         lax.all_to_all(as_sent(parts_tuple), "seq", split_axis=0, concat_axis=1, tiled=True),
         parts_tuple,
     )
-
-
-def to_owner(slab_rows):
-    return lax.all_to_all(slab_rows, "wshard", split_axis=0, concat_axis=0, tiled=True)
-
-
-def from_owner(slab_rows):
-    return lax.all_to_all(slab_rows, "wshard", split_axis=0, concat_axis=0, tiled=True)
-
-
-def all_quarters(slab_rows):
-    return lax.all_gather(slab_rows, "seq", axis=0, tiled=True)
-
-
-def pair_sum(partial_sum):
-    return partial_sum + from_partner(partial_sum, "wshard", 0)
-
-
-def quarter_sum(partial_sum):
-    return lax.psum_scatter(partial_sum, "seq", scatter_dimension=0, tiled=True)
-
-
-def expert_view(slab_rows):
-    return all_quarters(slab_rows)
-
-
-def hidden_total(partial_sum):
-    return quarter_sum(pair_sum(partial_sum))
 
 
 def attend_forward(query_head, key_head, value_head, block_row, score_scale):
@@ -207,31 +179,37 @@
     tok_count = inputs.shape[1]
     model_width = inputs.shape[2]
     exp_count = centroid.shape[0]
-    slot_most = max(2, 3 * tok_count // (2 * exp_count))
-    local_capacity = max(1, 9 * tok_count // (8 * exp_count))
+    seq_size = lax.axis_size("seq")
+    wshard_size = lax.axis_size("wshard")
+    slots = max(1, 9 * tok_count // (8 * exp_count))
     score_scale = HEAD ** (-0.5)
-    half_width = model_width // 2
-    pair_bit = lax.axis_index("wshard") % 2
-    full_qkv, full_out, full_gain_one, full_gain_two = (
-        lax.all_gather(qkv_weight, "wshard", axis=0, tiled=True),
-        lax.all_gather(out_weight, "wshard", axis=0, tiled=True),
-        lax.all_gather(gain_one, "wshard", axis=0, tiled=True),
-        lax.all_gather(gain_two, "wshard", axis=0, tiled=True),
-    )
+    head_width = model_width // seq_size
+    seq_index = lax.axis_index("seq")
+    same_core = [list(range(core, wshard_size, 2)) for core in range(2)]
+
+    qkv_parts = qkv_weight.reshape(-1, 3, model_width)
+    qkv_own = lax.dynamic_slice_in_dim(qkv_parts, seq_index * head_width, head_width, 2)
+    qkv_heads = lax.all_gather(
+        qkv_own.reshape(-1, 3 * head_width), "wshard", axis=0, tiled=True
+    )
+    full_gain_one = lax.all_gather(gain_one, "wshard", axis=0, tiled=True)
+    full_gain_two = lax.all_gather(gain_two, "wshard", axis=0, tiled=True)
     gain_first = full_gain_one.astype(jnp.float32)
     gain_second = full_gain_two.astype(jnp.float32)
     tokens_in = inputs[0].astype(jnp.float32)
     normed_one = norm_rows(tokens_in, gain_first).astype(jnp.bfloat16)
-    projected = jnp.dot(normed_one, full_qkv, preferred_element_type=jnp.float32).astype(
+    normed_all = lax.all_gather(normed_one, "seq", axis=0, tiled=True)
+    full_out = lax.all_gather(out_weight, "wshard", axis=0, tiled=True)
+    up_a, down_a, up_b, down_b = (
+        lax.all_gather(part[0], "seq", axis=0, tiled=True)
+        for part in (up_one, down_one, up_two, down_two)
+    )
+    projected = jnp.dot(normed_all, qkv_heads, preferred_element_type=jnp.float32).astype(
         jnp.bfloat16
     )
-    query_head, key_head, value_head = heads_layout(
-        (
-            projected[:, :model_width],
-            projected[:, model_width : 2 * model_width],
-            projected[:, 2 * model_width :],
-        )
-    )
+    query_head = projected[:, :head_width]
+    key_head = projected[:, head_width : 2 * head_width]
+    value_head = projected[:, 2 * head_width :]
     block_row = block_ids[0]
     mixed_head, log_total = attend_forward(query_head, key_head, value_head, block_row, score_scale)
     (mixed_tok,) = tokens_layout((mixed_head,))
@@ -248,75 +226,79 @@
     lower_tri = (positions[:, None] >= positions[None, :]).astype(jnp.bfloat16)
     running = jnp.dot(lower_tri, hot_low, preferred_element_type=jnp.float32)
     local_rank = (jnp.sum(jnp.where(expert_hot, running, 0.0), axis=1) - 1.0).astype(jnp.int32)
-    kept_mask = local_rank < local_capacity
+    kept_mask = local_rank < slots
     gate_val = jnp.where(kept_mask, sigmoid_val, 0.0)
-    slot_id = route_ids * slot_most + local_rank
-    slot_ids = jnp.arange(exp_count * slot_most, dtype=jnp.int32)
+    slot_id = route_ids * slots + local_rank
+    slot_ids = jnp.arange(exp_count * slots, dtype=jnp.int32)
     dispatch = ((slot_ids[:, None] == slot_id[None, :]) & kept_mask[None, :]).astype(jnp.bfloat16)
-
-    def spread_out(token_rows):
-        packed = jnp.dot(dispatch, token_rows, preferred_element_type=jnp.float32).astype(
-            jnp.bfloat16
-        )
-        packed = packed.reshape(exp_count, 1, slot_most, model_width)
-        doubled = jnp.broadcast_to(packed, (exp_count, 2, slot_most, model_width)).reshape(
-            2 * exp_count, slot_most, model_width
-        )
-        return to_owner(doubled).reshape(-1, model_width)
-
-    def gather_back(own_rows):
-        own_half = lax.dynamic_slice_in_dim(own_rows, pair_bit * half_width, half_width, 1)
-        returned = from_owner(own_half.reshape(2 * exp_count, slot_most, half_width))
-        paired = returned.reshape(exp_count, 2, slot_most, half_width)
-        joined = jnp.concatenate((paired[:, 0], paired[:, 1]), axis=2).reshape(
-            exp_count * slot_most, model_width
-        )
-        return dot_rows(dispatch, joined)
-
-    up_a, down_a, up_b, down_b = (up_one[0], down_one[0], up_two[0], down_two[0])
-    sent_own = spread_out(normed_two)
-    sent_all = expert_view(sent_own)
+    dy_rows = cotangent[0].astype(jnp.float32)
+
+    def exchange(slab):
+        return lax.all_to_all(
+            slab, "wshard", split_axis=0, concat_axis=0, axis_index_groups=same_core, tiled=True
+        )
+
+    both = jnp.concatenate((normed_two, (gate_val[:, None] * dy_rows).astype(jnp.bfloat16)), axis=1)
+    packed = jnp.dot(dispatch, both, preferred_element_type=jnp.float32).astype(jnp.bfloat16)
+    own_both = exchange(packed.reshape(exp_count, slots, 2 * model_width)).reshape(
+        exp_count * slots, 2 * model_width
+    )
+    pair_both = from_partner(own_both, "wshard", 0)
+    sent_all = jnp.concatenate((own_both[:, :model_width], pair_both[:, :model_width]), axis=0)
+    d_second_all = jnp.concatenate((own_both[:, model_width:], pair_both[:, model_width:]), axis=0)
+    own_rows = exp_count * slots
+
+    def pair_total(partial_sum):
+        other = from_partner(partial_sum, "wshard", 0)
+        return partial_sum + jnp.concatenate((other[own_rows:], other[:own_rows]), axis=0)
+
+    def add_rows(base, term):
+        return (base.astype(jnp.float32) + term).astype(jnp.bfloat16)
+
     pre_one = dot_last(sent_all, up_a)
     act_one = gelu_exact(pre_one).astype(jnp.bfloat16)
-    first_own = (
-        sent_own.astype(jnp.float32)
-        + hidden_total(jnp.dot(act_one, down_a, preferred_element_type=jnp.float32))
-    ).astype(jnp.bfloat16)
-    first_all = expert_view(first_own)
+    first_all = add_rows(
+        sent_all, pair_total(jnp.dot(act_one, down_a, preferred_element_type=jnp.float32))
+    )
     pre_two = dot_last(first_all, up_b)
     act_two = gelu_exact(pre_two).astype(jnp.bfloat16)
-    second_own = (
-        first_own.astype(jnp.float32)
-        + hidden_total(jnp.dot(act_two, down_b, preferred_element_type=jnp.float32))
-    ).astype(jnp.bfloat16)
-    returned_tok = gather_back(second_own)
+    second_part = jnp.dot(act_two, down_b, preferred_element_type=jnp.float32)
+    second_own = add_rows(
+        first_all[:own_rows],
+        second_part[:own_rows] + from_partner(second_part[own_rows:], "wshard", 0),
+    )
+    d_pre_two = gelu_back(pre_two, dot_last(d_second_all, down_b)).astype(jnp.bfloat16)
+    d_first_all = add_rows(
+        d_second_all, pair_total(jnp.dot(d_pre_two, up_b, preferred_element_type=jnp.float32))
+    )
+    d_pre_one = gelu_back(pre_one, dot_last(d_first_all, down_a)).astype(jnp.bfloat16)
+    d_sent_part = jnp.dot(d_pre_one, up_a, preferred_element_type=jnp.float32)
+    d_sent_own = add_rows(
+        d_first_all[:own_rows],
+        d_sent_part[:own_rows] + from_partner(d_sent_part[own_rows:], "wshard", 0),
+    )
+
+    def weight_grad(left, right):
+        return lax.psum_scatter(
+            dot_rows(left, right).astype(jnp.bfloat16), "seq", scatter_dimension=0, tiled=True
+        ).astype(jnp.float32)
+
+    grad_down_b = weight_grad(act_two, d_second_all)
+    grad_up_b = weight_grad(d_pre_two, first_all)
+    grad_down_a = weight_grad(act_one, d_first_all)
+    grad_up_a = weight_grad(d_pre_one, sent_all)
+
+    def give_back(rows):
+        return dot_rows(
+            dispatch,
+            exchange(rows.reshape(exp_count, slots, model_width)).reshape(own_rows, model_width),
+        )
+
+    returned_tok = give_back(second_own)
     layer_out = (hidden + gate_val[:, None] * returned_tok).astype(jnp.bfloat16)
-    dy_rows = cotangent[0].astype(jnp.float32)
     d_gate = jnp.where(kept_mask, jnp.sum(dy_rows * returned_tok, axis=1), 0.0)
     d_chosen = d_gate * sigmoid_val * (1.0 - sigmoid_val)
-    d_second_own = spread_out((gate_val[:, None] * dy_rows).astype(jnp.bfloat16))
-    d_second_all = expert_view(d_second_own)
-    d_pre_two = gelu_back(pre_two, dot_last(d_second_all, down_b)).astype(jnp.bfloat16)
-    d_first_own = (
-        d_second_own.astype(jnp.float32)
-        + hidden_total(jnp.dot(d_pre_two, up_b, preferred_element_type=jnp.float32))
-    ).astype(jnp.bfloat16)
-    d_first_all = expert_view(d_first_own)
-    d_pre_one = gelu_back(pre_one, dot_last(d_first_all, down_a)).astype(jnp.bfloat16)
-    d_sent_own = (
-        d_first_own.astype(jnp.float32)
-        + hidden_total(jnp.dot(d_pre_one, up_a, preferred_element_type=jnp.float32))
-    ).astype(jnp.bfloat16)
-    grad_stack = jnp.stack(
-        (
-            dot_rows(d_pre_one, sent_all),
-            dot_rows(act_one, d_first_all),
-            dot_rows(d_pre_two, first_all),
-            dot_rows(act_two, d_second_all),
-        ),
-        axis=1,
-    )
-    d_sent_tok = gather_back(d_sent_own)
+    d_sent_tok = give_back(d_sent_own)
     centroid_tok = jnp.dot(hot_low, centroid, preferred_element_type=jnp.float32)
     d_normed_two = d_sent_tok + d_chosen[:, None] * centroid_tok
     centroid_term = lax.dot_general(
@@ -326,7 +308,6 @@
         precision=lax.Precision.HIGHEST,
         preferred_element_type=jnp.float32,
     )
-    grad_centroid = lax.psum(centroid_term, ("seq", "wshard"))
     norm_two_back = jax.vjp(norm_rows, hidden, gain_second)[1]
     d_hidden_norm, d_gain_second = norm_two_back(d_normed_two)
     d_hidden = dy_rows + d_hidden_norm
@@ -337,25 +318,32 @@
     d_query, d_key, d_value = attend_backward(
         query_head, key_head, value_head, block_row, log_total, d_mixed_head, score_scale
     )
-    d_query_tok, d_key_tok, d_value_tok = tokens_layout((d_query, d_key, d_value))
-    d_projected = jnp.concatenate((d_query_tok, d_key_tok, d_value_tok), axis=1)
-    grad_qkv_full = dot_rows(normed_one, d_projected)
-    d_normed_one = dot_last(d_projected, full_qkv)
+    d_projected = jnp.concatenate((d_query, d_key, d_value), axis=1)
+    grad_qkv_heads = dot_rows(normed_all, d_projected)
+    d_normed_part = dot_last(d_projected, qkv_heads)
+    d_normed_one = lax.psum_scatter(
+        d_normed_part.astype(jnp.bfloat16), "seq", scatter_dimension=0, tiled=True
+    ).astype(jnp.float32)
     norm_one_back = jax.vjp(norm_rows, tokens_in, gain_first)[1]
     d_tokens_norm, d_gain_first = norm_one_back(d_normed_one)
     input_grad = (d_hidden + d_tokens_norm).astype(jnp.bfloat16)
-    qkv_part, out_part, gain_first_part, gain_second_part = (
-        lax.psum_scatter(grad_qkv_full, "wshard", scatter_dimension=0, tiled=True),
-        lax.psum_scatter(grad_out_full, "wshard", scatter_dimension=0, tiled=True),
-        lax.psum_scatter(d_gain_first, "wshard", scatter_dimension=0, tiled=True),
-        lax.psum_scatter(d_gain_second, "wshard", scatter_dimension=0, tiled=True),
-    )
-    grad_qkv, grad_out, grad_gain_one, grad_gain_two = (
-        lax.psum(qkv_part.astype(jnp.bfloat16), "seq").astype(jnp.float32),
-        lax.psum(out_part.astype(jnp.bfloat16), "seq").astype(jnp.float32),
-        lax.psum(gain_first_part.astype(jnp.bfloat16), "seq").astype(jnp.float32),
-        lax.psum(gain_second_part.astype(jnp.bfloat16), "seq").astype(jnp.float32),
-    )
+    qkv_sum = lax.psum_scatter(grad_qkv_heads, "wshard", scatter_dimension=0, tiled=True)
+    qkv_all = lax.all_gather(qkv_sum.astype(jnp.bfloat16), "seq", axis=0, tiled=False)
+    qkv_rows = qkv_sum.shape[0]
+    grad_qkv = (
+        jnp.transpose(qkv_all.reshape(seq_size, qkv_rows, 3, head_width), (1, 2, 0, 3))
+        .reshape(qkv_rows, 3 * model_width)
+        .astype(jnp.float32)
+    )
+    out_part = lax.psum_scatter(grad_out_full, "wshard", scatter_dimension=0, tiled=True)
+    grad_out = lax.psum(out_part.astype(jnp.bfloat16), "seq").astype(jnp.float32)
+    small = jnp.concatenate((d_gain_first[None], d_gain_second[None], centroid_term), axis=0)
+    small = lax.psum(small, ("seq", "wshard"))
+    gain_rows = gain_one.shape[0]
+    gain_at = lax.axis_index("wshard") * gain_rows
+    grad_gain_one = lax.dynamic_slice_in_dim(small[0], gain_at, gain_rows, 0)
+    grad_gain_two = lax.dynamic_slice_in_dim(small[1], gain_at, gain_rows, 0)
+    grad_centroid = small[2:]
     return (
         layer_out[None],
         input_grad[None],
@@ -364,10 +352,10 @@
         grad_gain_one,
         grad_gain_two,
         grad_centroid,
-        grad_stack[:, 0][None],
-        grad_stack[:, 1][None],
-        grad_stack[:, 2][None],
-        grad_stack[:, 3][None],
+        grad_up_a[None],
+        grad_down_a[None],
+        grad_up_b[None],
+        grad_down_b[None],
     )
 
 

time: 1430 us -> 803 us (0.56)
  waiting for transfers between devices: 857 us -> 378 us
  blocking collectives: 176 us -> 105 us
  other arithmetic: 82.1 us -> 49.3 us
  starting transfers between devices: 47.5 us -> 25.4 us
  matrix products: 190 us -> 172 us
    reduce_scatter x5 -> x6, waiting for transfers between devices: 478 us -> 105 us  [the longest x4 62.4 us: weight_grad(): lax.psum_scatter(dot_rows(left, right).astype(jnp.bfloat16), 'seq', scatt...]
    all_gather x6 -> x7, waiting for transfers between devices: 258 us -> 165 us  [the longest x4 118 us: local(): lax.all_gather(part[0], 'seq', axis=0, tiled=True)]
    all_to_all x3 -> x1, blocking collectives: 90.1 us -> 33.2 us  [exchange(): lax.all_to_all(slab, 'wshard', split_axis=0, concat_axis=0, axis_index_gr...]
    ppermute x4 -> x5, waiting for transfers between devices: 57.4 us -> 6.15 us  [from_partner(): lax.ppermute(shard, axis, [(i, i ^ 1 << distance) for i in range(lax.axis...]
    reduce_scatter x1, waiting for transfers between devices: 0.01 us -> 47.1 us  [local(): lax.psum_scatter(grad_out_full, 'wshard', scatter_dimension=0, tiled=True)]
    add x5 -> x1, other arithmetic: 33.6 us -> 0.01 us  [local(): slot_id = route_ids * slots + local_rank]
    all_to_all x4 -> x1, waiting for transfers between devices: 18.6 us -> 0.01 us  [heads_layout(): lax.all_to_all(as_sent(parts_tuple), 'seq', split_axis=1, concat_axis=0,...]
    psum x2 -> x1, blocking collectives: 52.8 us -> 41.6 us  [local(): small = lax.psum(small, ('seq', 'wshard'))]
  transfers between devices with their start and end apart: 26 -> 24, of which waited for: 21 -> 15; matrix products, arithmetic and copies ran while one was open for 16% -> 29% of each run, Pallas kernels for 0% -> 0%
where the time goes in v1:
time: 803 us; the launch traced here: 791 us
  waiting for transfers between devices  378 us (47%)
  matrix products  172 us (21%)
  blocking collectives  105 us (13%)
  other arithmetic  49.3 us (6%)
  local copies, waits for them, and re-layouts  37.8 us (5%)
  starting transfers between devices  25.4 us (3%)
  between operations  15.4 us (2%)
  loops' own time  8.28 us (1%)
    all_gather x4, waiting for transfers between devices, local(): lax.all_gather(part[0], 'seq', axis=0, tiled=True)  118 us
    reduce_scatter x4, waiting for transfers between devices, weight_grad(): lax.psum_scatter(dot_rows(left, right).astype(jnp.bfloat16), 'seq', scatt...  62.4 us
    dot_general x7, matrix products, dot_last(): lax.dot_general(left_mat, right_mat, (((1,), (1,)), ((), ())), preferred_...  54.7 us
    reduce_scatter x1, waiting for transfers between devices, local(): lax.psum_scatter(grad_out_full, 'wshard', scatter_dimension=0, tiled=True)  47.1 us
    psum x1, blocking collectives, local(): small = lax.psum(small, ('seq', 'wshard'))  41.6 us
    dot_general x8, matrix products, dot_rows(): lax.dot_general(left_mat, right_mat, (((0,), (0,)), ((), ())), preferred_...  38.8 us
    all_gather x1, waiting for transfers between devices, local(): normed_all = lax.all_gather(normed_one, 'seq', axis=0, tiled=True)  36.8 us
    reduce_scatter x1, waiting for transfers between devices, local(): lax.psum_scatter(grad_qkv_heads, 'wshard', scatter_dimension=0, tiled=True)  36.3 us
  transfers between devices with their start and end apart: 24, of which 15 were waited for; matrix products, arithmetic and copies ran while one was open for 29% of the time, Pallas kernels for 0%

profile of v1, /device:TPU:14, one launch (start us, length us, event | category | flops | bytes accessed | tf_op | source)
XLA Modules:
  0.0 791.2 jit_solution(11065188266168961729)
XLA Ops:
  9.5 9.2 %all-gather.5 = bf16[8,1,128]{2,1,0:T(2,128)(2,1)S(1)} all-gather(bf16[1,1,128]{2,1,0:T(2,128)(2,1)} %bitcast.284), channel_id=1, replica_groups=mesh['seq'=4,'wshard'=8] {'wshard'}, dimensions={0}, use_global_device_ids=true | all-gather | bytes 2304 | tf_op jit(solution)/shard_map/all_gather | solution.py:195
  27.0 10.1 %all-gather.17.cloned.1.call-done = bf16[1024,768]{0,1:T(8,128)(2,1)} async-done(((bf16[128,768]{0,1:T(8,128)(2,1)}), bf16[1024,768]{0,1:T(8,128)(2,1)}) %all-gather.17.cloned.1.call-update) | async-done | bytes 1572880 | tf_op jit(solution)/shard_map/all_gather | solution.py:192
  37.1 36.8 %all-gather.15.cloned.1.call-done = bf16[1024,1024]{1,0:T(8,128)(2,1)} async-done(((bf16[256,1024]{1,0:T(8,128)(2,1)}), bf16[1024,1024]{1,0:T(8,128)(2,1)}) %all-gather.15.cloned.1.call-update) | async-done | bytes 2097168 | tf_op jit(solution)/shard_map/all_gather | solution.py:201
  73.9 3.9 convolution_convert_fusion.6
  79.5 24.5 %while.27 = (s32[]{:T(128)}, bf16[2,512,256]{2,1,0:T(8,128)(2,1)}, f32[2,4,512]{2,1,0:T(4,128)S(1)}, s32[1,1024]{1,0:T(1,128)S(1)}, s32[2]{0:T(128)S(1)}, /*inde...) while((s32[]{:T(128)}, bf16[2,512,256]{2,1,0:T(8,128)(2,1)}, ...), condition=%wide.region_5.6_spmd, body=%wide.region_2.5_spmd.sunk | while | flops 562690048 | bytes 30485168 | solution.py:99
  87.8 3.1 fusion.189
  104.0 5.1 all-to-all-start
  109.0 9.0 %all-gather.6 = bf16[8,1,128]{2,1,0:T(2,128)(2,1)S(1)} all-gather(bf16[1,1,128]{2,1,0:T(2,128)(2,1)S(1)} %bitcast.285), channel_id=1, replica_groups=mesh['seq'=4,'wshard'=8] {'wshard'}, dimensions={0}, use_global_device_ids=true | all-gather | bytes 2304 | tf_op jit(solution)/shard_map/all_gather | solution.py:196
  123.3 33.2 %all_to_all.53 = bf16[4,72,2048]{2,1,0:T(8,128)(2,1)S(1)} all-to-all(bf16[4,72,2048]{2,1,0:T(8,128)(2,1)S(1)} %bitcast.260), channel_id=1, replica_groups={{0,2,4,6},{1,3,5,7},{8,10,12,14},{9,11,13,15},{16,18,20,22},{17,19,21,2..., dimensions={0} | all-to-all | bytes 2359296 | tf_op jit(solution)/shard_map/all_to_all | solution.py:237
  159.5 16.9 %multiply_convert_fusion.2 = (bf16[576,2048]{1,0:T(8,128)(2,1)}, f32[576,2048]{1,0:T(8,128)}, f32[576,2048]{1,0:T(8,128)}) fusion(bf16[1,2048,1024]{2,1,0:T(8,128)(2,1)} %all-gather.21.cloned.1.call-done, bf16[288,1024]{1,0:T(8,128)(2,1)S(1)} %get-tuple-element.269, bf16[288,1024]{1,0:T(8,128)(2,1)S(1)} %get-tuple-element.267), kind=kOutput, calls=%fused_computation.52 | convolution fusion | flops 2494955520 | bytes 17170432 | tf_op jit(solution)/shard_map/dot_general | solution.py:47
  176.4 36.4 %all-gather.23.cloned.1.call-done = bf16[1,2048,1024]{2,1,0:T(8,128)(2,1)} async-done(((bf16[1,512,1024]{2,1,0:T(8,128)(2,1)}), bf16[1,2048,1024]{2,1,0:T(8,128)(2,1)}) %all-gather.23.cloned.1.call-update) | async-done | bytes 4194320 | tf_op jit(solution)/shard_map/all_gather | solution.py:204
  212.7 5.1 fusion.43
  217.9 4.5 collective-permute-done.1
  223.5 43.5 %all-gather.25.cloned.1.call-done = bf16[1,2048,1024]{2,1,0:T(8,128)(2,1)} async-done(((bf16[1,512,1024]{2,1,0:T(8,128)(2,1)}), bf16[1,2048,1024]{2,1,0:T(8,128)(2,1)}) %all-gather.25.cloned.1.call-update) | async-done | bytes 4194320 | tf_op jit(solution)/shard_map/all_gather | solution.py:204
  267.0 16.8 %multiply_convert_fusion.1 = (bf16[576,2048]{1,0:T(8,128)(2,1)}, f32[576,2048]{1,0:T(8,128)}, f32[576,2048]{1,0:T(8,128)}) fusion(bf16[576,1024]{1,0:T(8,128)(2,1)S(1)} %fusion.54, bf16[1,2048,1024]{2,1,0:T(8,128)(2,1)} %all-gather.25.cloned.1.call-done), kind=kOutput, calls=%fused_computation.39 | convolution fusion | flops 2492596224 | bytes 17170432 | tf_op jit(solution)/shard_map/dot_general | solution.py:47
  283.8 37.7 %all-gather.27.cloned.1.call-done = bf16[1,2048,1024]{2,1,0:T(8,128)(2,1)} async-done(((bf16[1,512,1024]{2,1,0:T(8,128)(2,1)}), bf16[1,2048,1024]{2,1,0:T(8,128)(2,1)}) %all-gather.27.cloned.1.call-update) | async-done | bytes 4194320 | tf_op jit(solution)/shard_map/all_gather | solution.py:204
  321.5 8.6 %add_convert_fusion.1 = bf16[576,2048]{1,0:T(8,128)(2,1)S(1)} fusion(f32[576,2048]{1,0:T(8,128)} %get-tuple-element.250, f32[576,2048]{1,0:T(8,128)} %get-tuple-element.276, bf16[1,2048,1024]{2,1,0:T(8,128)(2,1)} %all-gather.27.cloned.1.call-done, bf16[288,1024]{1,0:T(8,128)(2,1)S(1)} %get-tuple-element.268, bf16[288,1024]{1,0:T(8,128)(2,1)S(1)} %copy-done.26), kind=kOutput, calls=%fused_computation.38 | convolution fusion | flops 2434793472 | bytes 17170432 | tf_op jit(solution)/shard_map/dot_general | solution.py:47
  330.1 4.1 fusion.37
  334.3 5.1 convolution_convert_fusion.1
  339.4 5.3 fusion.35
  350.3 6.7 add_convert_fusion
  362.5 5.3 all-to-all-start.2
  370.7 10.0 %all-to-all-done.2 = bf16[4,72,1024]{2,1,0:T(8,128)(2,1)S(1)} async-done(((bf16[4,72,1024]{2,1,0:T(8,128)(2,1)}), bf16[4,72,1024]{2,1,0:T(8,128)(2,1)S(1)}, u32[]{:S(2)}, u32[]{:S(2)}) %all-to-all-start.2) | async-done | bytes 589856 | tf_op jit(solution)/shard_map/all_to_all | solution.py:237
  381.5 7.4 all-to-all-start.3
  392.8 8.2 %all-to-all-done.3 = bf16[4,72,1024]{2,1,0:T(8,128)(2,1)} async-done(((bf16[4,72,1024]{2,1,0:T(8,128)(2,1)}), bf16[4,72,1024]{2,1,0:T(8,128)(2,1)}, u32[]{:S(2)}, u32[]{:S(2)}) %all-to-all-start.3) | async-done | bytes 589856 | tf_op jit(solution)/shard_map/all_to_all | solution.py:237
  408.7 5.9 all-to-all-start.4
  414.6 6.9 convolution_convert_fusion
  422.9 64.8 %while.28 = (s32[]{:T(128)}, f32[1024,4,64]{0,2,1:T(8,128)S(1)}, f32[1024,4,64]{0,2,1:T(8,128)}, bf16[2,512,256]{2,1,0:T(8,128)(2,1)}, s32[2]{0:T(128)S(1)}, /*i...) while((s32[]{:T(128)}, f32[1024,4,64]{0,2,1:T(8,128)S(1)}, ...), condition=%wide.region_15.16_spmd.clone, body=%wide.region_13.15_spmd.clone.sunk | while | flops 1375729664 | bytes 118819648 | solution.py:155
  426.8 4.8 fusion.200
  433.3 5.8 multiply_reduce_fusion.5
  446.4 3.2 fusion.201
  449.6 5.9 fusion.202
  459.2 4.8 fusion.200
  465.6 5.9 multiply_reduce_fusion.5
  478.4 3.1 fusion.201
  481.6 6.2 fusion.202
  489.8 4.7 convolution_convert_fusion.5
  494.6 6.9 convolution_convert_fusion.3
  505.4 7.1 convolution_convert_fusion.2
  512.6 5.3 fusion.84
  524.2 6.4 reduce-scatter.8.cloned.1.call-done
  533.7 41.6 %psum.15 = f32[6,1024]{1,0:T(8,128)S(1)} all-reduce(f32[6,1024]{1,0:T(8,128)S(1)} %pad_maximum_fusion.9), channel_id=1, replica_groups=mesh['seq'=4,'wshard'=8] {'seq','wshard'}, use_global_device_ids=true, to_apply=%region_24.25 | all-reduce | flops 6144 | bytes 49152 | tf_op jit(solution)/shard_map/psum | solution.py:341
  578.9 7.9 %reduce-scatter.14.cloned.1.call-done = bf16[512,1024]{1,0:T(8,128)(2,1)} async-done(((bf16[2048,1024]{1,0:T(8,128)(2,1)}), bf16[512,1024]{1,0:T(8,128)(2,1)}) %reduce-scatter.14.cloned.1.call-update) | async-done | bytes 1048592 | tf_op jit(solution)/shard_map/reduce_scatter | solution.py:282
  589.6 47.1 %reduce-scatter.12.cloned.1.call-done = f32[128,1024]{1,0:T(8,128)} async-done(((f32[1024,1024]{1,0:T(8,128)}), f32[128,1024]{1,0:T(8,128)}) %reduce-scatter.12.cloned.1.call-update) | async-done | bytes 524304 | tf_op jit(solution)/shard_map/reduce_scatter | solution.py:338
  638.5 54.5 %reduce-scatter.16.cloned.1.call-done = bf16[512,1024]{1,0:T(8,128)(2,1)} async-done(((bf16[2048,1024]{1,0:T(8,128)(2,1)}), bf16[512,1024]{1,0:T(8,128)(2,1)}) %reduce-scatter.16.cloned.1.call-update) | async-done | bytes 1048592 | tf_op jit(solution)/shard_map/reduce_scatter | solution.py:282
  695.8 36.3 %reduce-scatter.10.cloned.1.call-done = f32[128,768]{1,0:T(8,128)} async-done(((f32[1024,768]{1,0:T(8,128)}), f32[128,768]{1,0:T(8,128)}) %reduce-scatter.10.cloned.1.call-update) | async-done | bytes 393232 | tf_op jit(solution)/shard_map/reduce_scatter | solution.py:330
  733.1 12.4 %all-gather.4 = bf16[512,768]{1,0:T(8,128)(2,1)S(1)} all-gather(bf16[128,768]{1,0:T(8,128)(2,1)S(1)} %convert_element_type.235), channel_id=6, replica_groups=mesh['seq'=4,'wshard'=8] {'seq'}, dimensions={0}, use_global_device_ids=true | all-gather | bytes 983040 | tf_op jit(solution)/shard_map/all_gather | solution.py:331
  748.1 34.3 %all-reduce.2.cloned.1.call-done = bf16[128,1024]{1,0:T(8,128)(2,1)} async-done(((bf16[128,1024]{1,0:T(8,128)(2,1)}), bf16[128,1024]{1,0:T(8,128)(2,1)}) %all-reduce.2.cloned.1.call-update) | async-done | bytes 262160 | tf_op jit(solution)/shard_map/psum | solution.py:339
  (325 shorter events, 118.7 us)
Async XLA Ops:
  7.2 115.0 %copy-start = (bf16[4,1024]{1,0:T(4,128)(2,1)S(1)}, bf16[4,1024]{1,0:T(4,128)(2,1)}, u32[]{:S(2)}) copy-start(bf16[4,1024]{1,0:T(4,128)(2,1)} %param.24) | copy-start | bytes 24580
  7.2 29.9 %all-gather.17.cloned.1.call-start = ((), (), s32[]{:S(2)}) async-start(), calls=%async_computation.13 | async-start | bytes 1769472 | tf_op jit(solution)/shard_map/all_gather | solution.py:192
  9.5 64.4 %all-gather.15.cloned.1.call-start = ((), (), s32[]{:S(2)}) async-start(), calls=%async_computation.12 | async-start | bytes 2621440 | tf_op jit(solution)/shard_map/all_gather | solution.py:201
  24.5 94.0 %all-gather.19.cloned.1.call-start = ((), (), s32[]{:S(2)}) async-start(), calls=%async_computation.14 | async-start | bytes 2359296 | tf_op jit(solution)/shard_map/all_gather | solution.py:202
  25.2 134.3 %all-gather.21.cloned.1.call-start = ((), (), s32[]{:S(2)}) async-start(), calls=%async_computation.23 | async-start | bytes 5242880 | tf_op jit(solution)/shard_map/all_gather | solution.py:204
  25.8 187.0 %all-gather.23.cloned.1.call-start = ((), (), s32[]{:S(2)}) async-start(), calls=%async_computation.24 | async-start | bytes 5242880 | tf_op jit(solution)/shard_map/all_gather | solution.py:204
  26.4 240.7 %all-gather.25.cloned.1.call-start = ((), (), s32[]{:S(2)}) async-start(), calls=%async_computation.25 | async-start | bytes 5242880 | tf_op jit(solution)/shard_map/all_gather | solution.py:204
  27.0 52.5 %copy-start.34 = (s32[1,1024]{1,0:T(1,128)S(1)}, s32[1,1024]{1,0:T(1,128)}, u32[]{:S(2)}) copy-start(s32[1,1024]{1,0:T(1,128)} %param.19) | copy-start | bytes 12292
  79.5 29.5 %copy-start.68 = (bf16[128]{0:T(256)(128)(2,1)S(1)}, bf16[128]{0:T(256)(128)(2,1)}, u32[]{:S(2)}) copy-start(bf16[128]{0:T(256)(128)(2,1)} %param.23) | copy-start | bytes 772
  79.5 38.5 %copy-start.50 = (s32[1,256,1]{1,2,0:T(1,128)S(1)}, s32[1,256,1]{1,2,0:T(1,128)}, u32[]{:S(2)}) copy-start(s32[1,256,1]{1,2,0:T(1,128)} %param.18) | copy-start | bytes 3076
  79.5 39.0 %copy-start.6 = (bf16[1,256,1024]{2,1,0:T(8,128)(2,1)S(1)}, bf16[1,256,1024]{2,1,0:T(8,128)(2,1)}, u32[]{:S(2)}) copy-start(bf16[1,256,1024]{2,1,0:T(8,128)(2,1)} %param.17) | copy-start | bytes 1572868
  104.0 14.3 %all-to-all-start = ((bf16[4,256,256]{2,1,0:T(8,128)(2,1)}), bf16[4,256,256]{2,1,0:T(8,128)(2,1)S(1)}, u32[]{:S(2)}, u32[]{:S(2)}) async-start(bf16[4,256,256]{2,1,0:T(8,128)(2,1)} %bitcast.14), calls=%async_computation | async-start | bytes 1048576 | tf_op jit(solution)/shard_map/all_to_all | solution.py:63
  109.0 212.5 %all-gather.27.cloned.1.call-start = ((), (), s32[]{:S(2)}) async-start(), calls=%async_computation.26 | async-start | bytes 5242880 | tf_op jit(solution)/shard_map/all_gather | solution.py:204
  121.1 35.4 %copy-start.48 = (f32[256]{0:T(256)}, f32[256]{0:T(256)S(1)}, u32[]{:S(2)}) copy-start(f32[256]{0:T(256)S(1)} %broadcast_multiply_fusion) | copy-start | bytes 3076
  121.4 36.3 %copy-start.54 = (f32[256]{0:T(256)}, f32[256]{0:T(256)S(1)}, u32[]{:S(2)}) copy-start(f32[256]{0:T(256)S(1)} %fusion.103) | copy-start | bytes 3076
  122.5 36.9 %copy-start.58 = (f32[256]{0:T(256)}, f32[256]{0:T(256)S(1)}, u32[]{:S(2)}) copy-start(f32[256]{0:T(256)S(1)} %fusion.68) | copy-start | bytes 3076
  122.5 34.0 %copy-start.64 = (f32[256]{0:T(256)}, f32[256]{0:T(256)S(1)}, u32[]{:S(2)}) copy-start(f32[256]{0:T(256)S(1)} %get-tuple-element.253) | copy-start | bytes 3076
  122.5 36.9 %copy-start.66 = (pred[256]{0:T(512)(128)(4,1)}, pred[256]{0:T(512)(128)(4,1)S(1)}, u32[]{:S(2)}) copy-start(pred[256]{0:T(512)(128)(4,1)S(1)} %get-tuple-element.254) | copy-start | bytes 772
  156.5 2.8 collective-permute-start
  156.5 362.1 %reduce-scatter.18.cloned.1.call-start = ((), (), s32[]{:S(2)}) async-start(), calls=%async_computation.21 | async-start | bytes 5242880 | tf_op jit(solution)/shard_map/reduce_scatter | solution.py:282
  157.7 65.0 %copy-start.22 = (bf16[288,1024]{1,0:T(8,128)(2,1)}, bf16[288,1024]{1,0:T(8,128)(2,1)S(1)}, u32[]{:S(2)}) copy-start(bf16[288,1024]{1,0:T(8,128)(2,1)S(1)} %get-tuple-element.267) | copy-start | bytes 1769476
  159.4 63.3 %copy-start.24 = (bf16[288,1024]{1,0:T(8,128)(2,1)}, bf16[288,1024]{1,0:T(8,128)(2,1)S(1)}, u32[]{:S(2)}) copy-start(bf16[288,1024]{1,0:T(8,128)(2,1)S(1)} %get-tuple-element.269) | copy-start | bytes 1769476
  159.5 187.7 %copy-start.27 = (bf16[288,1024]{1,0:T(8,128)(2,1)}, bf16[288,1024]{1,0:T(8,128)(2,1)S(1)}, u32[]{:S(2)}) copy-start(bf16[288,1024]{1,0:T(8,128)(2,1)S(1)} %get-tuple-element.268) | copy-start | bytes 1769476
  217.8 4.6 collective-permute-start.1
  223.5 98.0 %copy-start.26 = (bf16[288,1024]{1,0:T(8,128)(2,1)S(1)}, bf16[288,1024]{1,0:T(8,128)(2,1)}, u32[]{:S(2)}) copy-start(bf16[288,1024]{1,0:T(8,128)(2,1)} %get-tuple-element.266) | copy-start | bytes 1769476
  334.3 11.1 %collective-permute-start.3 = (f32[576,1024]{1,0:T(8,128)}, f32[576,1024]{1,0:T(8,128)}, u32[]{:S(2)}, u32[]{:S(2)}) collective-permute-start(f32[576,1024]{1,0:T(8,128)} %fusion.37), channel_id=1, source_target_pairs={{0,1},{1,0},{2,3},{3,2},{4,5},{5,4},{6,7},{7,6},{8,9},{9,8},{10,11... | collective-permute-start | bytes 7077896 | tf_op jit(solution)/shard_map/ppermute | solution.py:22
  344.8 16.6 %collective-permute-start.2 = (f32[288,1024]{1,0:T(8,128)S(1)}, f32[288,1024]{1,0:T(8,128)S(1)}, u32[]{:S(2)}, u32[]{:S(2)}) collective-permute-start(f32[288,1024]{1,0:T(8,128)S(1)} %slice.89), channel_id=1, source_target_pairs={{0,1},{1,0},{2,3},{3,2},{4,5},{5,4},{6,7},{7,6},{8,9},{9,8},{10,11... | collective-permute-start | bytes 3538952 | tf_op jit(solution)/shard_map/ppermute | solution.py:22
  360.9 6.8 collective-permute-start.4
  362.5 29.0 %copy-start.59 = (f32[256]{0:T(256)S(1)}, f32[256]{0:T(256)}, u32[]{:S(2)}) copy-start(f32[256]{0:T(256)} %copy-done.58) | copy-start | bytes 3076
  362.5 29.0 %copy-start.51 = (s32[1,256,1]{1,2,0:T(1,128)S(1)}, s32[1,256,1]{1,2,0:T(1,128)}, u32[]{:S(2)}) copy-start(s32[1,256,1]{1,2,0:T(1,128)} %param.18) | copy-start | bytes 3076
  362.5 38.6 %copy-start.5 = (f32[256,1024]{1,0:T(8,128)S(1)}, f32[256,1024]{1,0:T(8,128)}, u32[]{:S(2)}) copy-start(f32[256,1024]{1,0:T(8,128)} %copy-done.4) | copy-start | bytes 3145732
  362.5 38.6 %copy-start.45 = (f32[8,1,128]{2,1,0:T(1,128)S(1)}, f32[8,1,128]{2,1,0:T(1,128)}, u32[]{:S(2)}) copy-start(f32[8,1,128]{2,1,0:T(1,128)} %copy-done.44) | copy-start | bytes 12292
  362.5 38.6 %copy-start.49 = (f32[256]{0:T(256)S(1)}, f32[256]{0:T(256)}, u32[]{:S(2)}) copy-start(f32[256]{0:T(256)} %copy-done.48) | copy-start | bytes 3076
  362.5 38.6 %copy-start.55 = (f32[256]{0:T(256)S(1)}, f32[256]{0:T(256)}, u32[]{:S(2)}) copy-start(f32[256]{0:T(256)} %copy-done.54) | copy-start | bytes 3076
  362.5 18.2 %all-to-all-start.2 = ((bf16[4,72,1024]{2,1,0:T(8,128)(2,1)}), bf16[4,72,1024]{2,1,0:T(8,128)(2,1)S(1)}, u32[]{:S(2)}, u32[]{:S(2)}) async-start(bf16[4,72,1024]{2,1,0:T(8,128)(2,1)} %bitcast.27), calls=%async_computation.2 | async-start | bytes 1179648 | tf_op jit(solution)/shard_map/all_to_all | solution.py:237
  370.7 32.7 %copy-start.63 = (f32[256]{0:T(256)S(1)}, f32[256]{0:T(256)}, u32[]{:S(2)}) copy-start(f32[256]{0:T(256)} %copy-done.62) | copy-start | bytes 3076
  370.7 32.7 %copy-start.65 = (f32[256]{0:T(256)S(1)}, f32[256]{0:T(256)}, u32[]{:S(2)}) copy-start(f32[256]{0:T(256)} %copy-done.64) | copy-start | bytes 3076
  381.5 19.6 %all-to-all-start.3 = ((bf16[4,72,1024]{2,1,0:T(8,128)(2,1)}), bf16[4,72,1024]{2,1,0:T(8,128)(2,1)}, u32[]{:S(2)}, u32[]{:S(2)}) async-start(bf16[4,72,1024]{2,1,0:T(8,128)(2,1)} %bitcast.31), calls=%async_computation.3 | async-start | bytes 1179648 | tf_op jit(solution)/shard_map/all_to_all | solution.py:237
  408.7 12.9 %all-to-all-start.4 = ((bf16[256,4,256]{2,0,1:T(8,128)(2,1)}), bf16[256,4,256]{2,0,1:T(8,128)(2,1)}, u32[]{:S(2)}, u32[]{:S(2)}) async-start(bf16[256,4,256]{2,0,1:T(8,128)(2,1)} %bitcast.189), calls=%async_computation.4 | async-start | bytes 1048576 | tf_op jit(solution)/shard_map/all_to_all | solution.py:55
  414.6 106.8 %reduce-scatter.20.cloned.1.call-start = ((), (), s32[]{:S(2)}) async-start(), calls=%async_computation.22 | async-start | bytes 5242880 | tf_op jit(solution)/shard_map/reduce_scatter | solution.py:282
  421.6 109.1 %reduce-scatter.8.cloned.1.call-start = ((), (), s32[]{:S(2)}) async-start(), calls=%async_computation.15 | async-start | bytes 2621440 | tf_op jit(solution)/shard_map/reduce_scatter | solution.py:324
  494.6 92.3 %reduce-scatter.14.cloned.1.call-start = ((), (), s32[]{:S(2)}) async-start(), calls=%async_computation.19 | async-start | bytes 5242880 | tf_op jit(solution)/shard_map/reduce_scatter | solution.py:282
  501.5 135.2 %reduce-scatter.12.cloned.1.call-start = ((), (), s32[]{:S(2)}) async-start(), calls=%async_computation.17 | async-start | bytes 4718592 | tf_op jit(solution)/shard_map/reduce_scatter | solution.py:338
  505.3 187.7 %reduce-scatter.16.cloned.1.call-start = ((), (), s32[]{:S(2)}) async-start(), calls=%async_computation.20 | async-start | bytes 5242880 | tf_op jit(solution)/shard_map/reduce_scatter | solution.py:282
  512.5 219.6 %reduce-scatter.10.cloned.1.call-start = ((), (), s32[]{:S(2)}) async-start(), calls=%async_computation.16 | async-start | bytes 3538944 | tf_op jit(solution)/shard_map/reduce_scatter | solution.py:330
  518.0 58.5 %copy-start.12 = (f32[256,1024]{1,0:T(8,128)S(1)}, f32[256,1024]{1,0:T(8,128)}, u32[]{:S(2)}) copy-start(f32[256,1024]{1,0:T(8,128)} %copy-done.11) | copy-start | bytes 3145732
  518.0 58.5 %copy-start.15 = (bf16[1,256,1024]{2,1,0:T(8,128)(2,1)S(1)}, bf16[1,256,1024]{2,1,0:T(8,128)(2,1)}, u32[]{:S(2)}) copy-start(bf16[1,256,1024]{2,1,0:T(8,128)(2,1)} %param.29) | copy-start | bytes 1572868
  518.0 264.4 %all-reduce.2.cloned.1.call-start = ((), (), s32[]{:S(2)}) async-start(), calls=%async_computation.18 | async-start | bytes 524288 | tf_op jit(solution)/shard_map/psum | solution.py:339
  (57 other events, 414.3 us)
Sparse Core Ops, SparseCore 0:
  10.2 26.9 all-gather.16
  39.5 34.2 all-gather.14
  75.5 30.0 all-gather.18
  107.3 51.1 all-gather.20
  160.1 52.5 all-gather.22
  214.4 52.5 all-gather.24
  268.9 52.5 all-gather.26
  339.5 52.7 reduce-scatter.17
  421.7 53.5 reduce-scatter.19
  494.7 35.9 reduce-scatter.7
  533.6 53.1 reduce-scatter.13
  589.0 47.6 reduce-scatter.11
  639.7 53.2 reduce-scatter.15
  695.1 36.9 reduce-scatter.9
  735.5 46.9 all-reduce.1
